TPU v7x, 32 devices: a whole 2x2x4 slice. The times are simulated.
32 devices in a mesh: groups: 2 (over y), rec: 4 (over z), attr: 4 (over x, core).
Axes of the slice: x: 2, y: 2, z: 4, core: 2. Of those that a mesh axis runs over, the one named last changes fastest.
Arguments:
- cells: bfloat16 [64, 49152], P(('groups', 'rec'), 'attr'), parts along dimension 0, may hold values from -1000 to 1000
- cotangent: bfloat16 [64, 49152], P(('groups', 'rec'), 'attr'), parts along dimension 0, may hold values from -6 to 6
- qkv_attr: bfloat16 [192, 576], replicated, may hold values from -8 to 8
- out_attr: bfloat16 [192, 192], replicated, may hold values from -0.4375 to 0.4375
- qkv_samp: bfloat16 [192, 576], replicated, may hold values from -8 to 8
- out_samp: bfloat16 [192, 192], replicated, may hold values from -0.4375 to 0.4375
- up_weight: bfloat16 [192, 768], replicated, may hold values from -0.4375 to 0.4375
- down_weight: bfloat16 [768, 192], replicated, may hold values from -0.21875 to 0.21875
- train_split: int32 [64], P('groups'), parts along dimension 0, may hold values from 0 to 1, as said below
Outputs:
- grad_cells: bfloat16 [64, 49152], P(('groups', 'rec'), 'attr'), parts along dimension 0
- grad_qkv_attr: float32 [384, 576], P('groups'), parts along dimension 0
- grad_out_attr: float32 [384, 192], P('groups'), parts along dimension 0
- grad_qkv_samp: float32 [384, 576], P('groups'), parts along dimension 0
- grad_out_samp: float32 [384, 192], P('groups'), parts along dimension 0
- grad_up: float32 [384, 768], P('groups'), parts along dimension 0
- grad_down: float32 [1536, 192], P('groups'), parts along dimension 0
There are 2 independent parts, one for each index of `groups`. A program takes and returns all parts, laid end to end along the dimension named above; an argument that names none is the same for every part. Nothing has to cross between parts.
Inputs may be any that keep to these rules, and one draw needn't show every extreme that they name: `train_split`: every table window has at least one training record.
All inputs are finite; a program needn't handle non-finite values.
Results may differ from a plain program's by a relative error of at most 0.018.
The roundings to bfloat16 on the way count: a program that leaves them out, or rounds other values in their place, can miss the bound.
Values may be sent and summed in bfloat16 or wider, within the bound.
A program may use at most 64 MiB of HBM per device.

v0:
```python
import functools
import math

import jax
import jax.numpy as jnp
import numpy as np
from jax import lax
from jax.experimental import pallas as pl
from jax.experimental.pallas import tpu as pltpu
from jax.sharding import PartitionSpec as P

E = 192
HEADS = 6
HD = E // HEADS
SCALE = 1.0 / math.sqrt(HD)
BLOCKS = 16
F32 = jnp.float32
BF16 = jnp.bfloat16
MESH = pl.DeviceIdType.MESH
NN = (((1,), (0,)), ((), ()))
NT = (((1,), (1,)), ((), ()))
TN = (((0,), (0,)), ((), ()))
VMEM = pl.BlockSpec(memory_space=pltpu.VMEM)


def dot(a, b, form=NN):
    return lax.dot_general(a, b, form, preferred_element_type=F32)


def place(sizes, order):
    index = np.arange(math.prod(sizes)).reshape(sizes).transpose(order).reshape(-1)
    there = np.empty_like(index)
    there[index] = np.arange(index.size)
    return jnp.asarray(there.astype(np.int32)[None, :])


def moved(where_ref, x):
    n = x.shape[0]
    hot = lax.broadcasted_iota(jnp.int32, (n, n), 0) == where_ref[...]
    return dot(jnp.where(hot, 1.0, 0.0).astype(BF16), x)


def norm(x):
    center = x - jnp.mean(x, axis=-1, keepdims=True)
    scale = lax.rsqrt(jnp.mean(center * center, axis=-1, keepdims=True) + 1e-05)
    return center * scale, scale


def norm_back(hat, scale, grad):
    return scale * (
        grad
        - jnp.mean(grad, axis=-1, keepdims=True)
        - hat * jnp.mean(grad * hat, axis=-1, keepdims=True)
    )


def head_mask(h):
    lane = lax.broadcasted_iota(jnp.int32, (1, E), 1)
    return jnp.where((lane >= h * HD) & (lane < (h + 1) * HD), 1.0, 0.0).astype(F32)


def attend(x_ref, qkv, out, qkv_s, p_s, acc, n, size, bias):
    normed = norm(x_ref[...].astype(F32))[0].astype(BF16)
    for t in range(3):
        qkv_s[t] = dot(normed, qkv[:, t * E:(t + 1) * E]).astype(BF16)
    acc[0] = jnp.zeros(acc.shape[1:], F32)

    def head(h, _):
        mask = head_mask(h)
        for b in range(n):
            rows = pl.ds(b * size, size)
            s = dot(qkv_s[0, rows] * mask.astype(BF16), qkv_s[1, rows], NT) * SCALE
            if bias is not None:
                s = jnp.where(bias[...] > 0, s, -1e30)
            e = jnp.exp(s - jnp.max(s, axis=-1, keepdims=True))
            p = e * (1.0 / jnp.sum(e, axis=-1, keepdims=True))
            p_s[b, h] = p
            acc[0, rows] += dot(p.astype(BF16), qkv_s[2, rows]) * mask
        return 0

    lax.fori_loop(0, HEADS, head, 0)
    mixed = acc[0].astype(BF16)
    return normed, mixed, (x_ref[...].astype(F32) + dot(mixed, out)).astype(BF16)


def attend_back(x, g, mixed, qkv, out, qkv_s, p_s, acc, dm_s, grads, first, n, size):
    dm_s[...] = dot(g, out, NT).astype(BF16)
    grads[first + 3] = dot(mixed, g, TN).astype(BF16)
    acc[...] = jnp.zeros(acc.shape, F32)

    def head(h, _):
        mask = head_mask(h)
        for b in range(n):
            rows = pl.ds(b * size, size)
            dm = dm_s[rows] * mask.astype(BF16)
            p = p_s[b, h]
            dp = dot(dm, qkv_s[2, rows], NT).astype(BF16).astype(F32)
            ds = (p * (dp - jnp.sum(dp * p, axis=-1, keepdims=True)) * SCALE).astype(BF16)
            acc[0, rows] += dot(ds, qkv_s[1, rows]) * mask
            acc[1, rows] += dot(ds, qkv_s[0, rows], TN) * mask
            acc[2, rows] += dot(p.astype(BF16), dm, TN)
        return 0

    lax.fori_loop(0, HEADS, head, 0)
    hat, scale = norm(x.astype(F32))
    normed = hat.astype(BF16)
    dn = None
    for t in range(3):
        d = acc[t].astype(BF16)
        grads[first + t] = dot(normed, d, TN).astype(BF16)
        part = dot(d, qkv[:, t * E:(t + 1) * E], NT)
        dn = part if dn is None else dn + part
    return (g.astype(F32) + norm_back(hat, scale, dn.astype(BF16).astype(F32))).astype(BF16)


def unpack_kernel(cells, cotangent, where, c_out, g_out, flat):
    rows = cells.shape[0]
    for a in range(cells.shape[1] // E):
        flat[a * rows:(a + 1) * rows] = cells[:, a * E:(a + 1) * E].astype(F32)
    c_out[...] = moved(where, flat[...].astype(BF16)).astype(BF16)
    for a in range(cells.shape[1] // E):
        flat[a * rows:(a + 1) * rows] = cotangent[:, a * E:(a + 1) * E].astype(F32)
    g_out[...] = flat[...].astype(BF16)


def attr_kernel(n, size, tokens, where_in, where_out, qkv, out, send, x_out, mixed_out, qkv_s, p_s, acc):
    x_out[...] = moved(where_in, tokens[...]).astype(BF16)
    _, mixed, result = attend(x_out, qkv, out[...], qkv_s, p_s, acc, n, size, None)
    mixed_out[...] = mixed
    send[...] = moved(where_out, result).astype(BF16)


def attr_back_kernel(n, size, tokens, where, x, mixed, qkv_s, p_s, qkv, out, send, grads, acc, dm_s):
    g = moved(where, tokens[...]).astype(BF16)
    send[...] = attend_back(
        x[...], g, mixed[...], qkv, out[...], qkv_s, p_s, acc, dm_s, grads, 0, n, size
    )


def middle_kernel(
    n, size, length, tokens, cots, where_x, where_g, where_back, split, qkv, out, up, down,
    send, grads, x_s, g_s, qkv_s, p_s, acc, dm_s, dn_s, bias,
):
    x_s[...] = moved(where_x, tokens[...]).astype(BF16)
    g_s[...] = moved(where_g, cots[...]).astype(BF16)
    row = lax.broadcasted_iota(jnp.int32, (size, size), 0)
    column = lax.broadcasted_iota(jnp.int32, (size, size), 1)
    same = None
    for s in range(size // length):
        low, high = s * length, (s + 1) * length
        inside = (row >= low) & (row < high) & (column >= low) & (column < high)
        same = inside if same is None else same | inside
    bias[...] = jnp.where(same & (split[...] > 0), 1.0, 0.0)
    _, mixed, second = attend(x_s, qkv, out[...], qkv_s, p_s, acc, n, size, bias)
    hat, scale = norm(second.astype(F32))
    normed = hat.astype(BF16)
    g = g_s[...]
    for c in range(up.shape[1] // E):
        w_up = up[:, c * E:(c + 1) * E]
        pre = dot(normed, w_up)
        cdf = 0.5 * (1.0 + lax.erf(pre * (1.0 / math.sqrt(2.0))))
        hidden = (pre * cdf).astype(BF16)
        slope = cdf + pre * (jnp.exp(pre * pre * -0.5) * (1.0 / math.sqrt(2.0 * math.pi)))
        dh = dot(g, down[c * E:(c + 1) * E], NT).astype(BF16).astype(F32)
        dpre = (dh * slope).astype(BF16)
        grads[4 + c] = dot(normed, dpre, TN).astype(BF16)
        grads[8 + c] = dot(hidden, g, TN).astype(BF16)
        part = dot(dpre, w_up, NT)
        if c == 0:
            dn_s[...] = part
        else:
            dn_s[...] += part
    dn = dn_s[...].astype(BF16).astype(F32)
    g = (g.astype(F32) + norm_back(hat, scale, dn)).astype(BF16)
    result = attend_back(
        x_s[...], g, mixed, qkv, out[...], qkv_s, p_s, acc, dm_s, grads, 0, n, size
    )
    send[...] = moved(where_back, result).astype(BF16)


def finish_kernel(factor, tokens, where, total, cells, qa, oa, qs, os, gu, gd, flat):
    rows = cells.shape[0]
    flat[...] = moved(where, tokens[...])
    for a in range(0, cells.shape[1] // E, 2):
        pair = [flat[(a + k) * rows:(a + k + 1) * rows] for k in range(2)]
        cells[:, a * E:(a + 2) * E] = jnp.concatenate(pair, axis=1).astype(BF16)

    def block(b):
        return total[b].astype(F32) * factor

    for ref, start in ((qs, 0), (qa, 12)):
        ref[...] = jnp.concatenate([block(start + t) for t in range(3)], axis=1)
    os[...] = block(3)
    oa[...] = block(15)
    gu[...] = jnp.concatenate([block(4 + c) for c in range(4)], axis=1)
    for c in range(4):
        gd[c * E:(c + 1) * E] = block(8 + c)


def greet(peers):
    barrier = pltpu.get_barrier_semaphore()
    for peer in peers:
        pl.semaphore_signal(barrier, inc=1, device_id=peer, device_id_type=MESH)
    pl.semaphore_wait(barrier, len(peers))


def position(axes):
    return tuple(lax.axis_index(a) for a in axes)


def shifts_of(axes):
    sizes = [lax.axis_size(a) for a in axes]
    return [s for s in np.ndindex(*sizes) if any(s)], sizes


def start_swap(axes, src, dst, send_sem, recv_sem):
    shifts, sizes = shifts_of(axes)
    me = position(axes)
    copies = []
    for k, shift in enumerate(shifts):
        to = tuple(lax.rem(m + d, n) for m, d, n in zip(me, shift, sizes))
        copy = pltpu.make_async_remote_copy(
            src_ref=src.at[to],
            dst_ref=dst.at[me],
            send_sem=send_sem.at[k],
            recv_sem=recv_sem.at[k],
            device_id=dict(zip(axes, to)),
            device_id_type=MESH,
        )
        copy.start()
        copies.append(copy)
    dst[me] = src[me]
    return copies


def peers_of(axes):
    shifts, sizes = shifts_of(axes)
    me = position(axes)
    return [
        dict(zip(axes, (lax.rem(m + d, n) for m, d, n in zip(me, s, sizes)))) for s in shifts
    ]


def swap_kernel(flows, *refs):
    n = len(flows)
    ins, outs, sems = refs[:n], refs[n:2 * n], refs[2 * n:]
    greeted = []
    names = []
    for axes in flows:
        if axes not in names:
            names.append(axes)
            greeted += peers_of(axes)
    greet(greeted)
    copies = []
    for f, axes in enumerate(flows):
        copies += start_swap(axes, ins[f], outs[f], sems[2 * f], sems[2 * f + 1])
    for copy in copies:
        copy.wait()


def swap(flows, arrays, number):
    counts = [math.prod(lax.axis_size(a) for a in axes) for axes in flows]
    return pl.pallas_call(
        functools.partial(swap_kernel, flows),
        out_shape=[jax.ShapeDtypeStruct(a.shape, a.dtype) for a in arrays],
        in_specs=[VMEM] * len(arrays),
        out_specs=[VMEM] * len(arrays),
        scratch_shapes=[pltpu.SemaphoreType.DMA((c,)) for c in counts for _ in range(2)],
        compiler_params=pltpu.CompilerParams(collective_id=number, has_side_effects=True),
    )(*arrays)


def total_kernel(cells, buf, cells_out, out, r1, r2, r3, s1, s2, c_send, c_recv, sems):
    rec, attr = lax.axis_index("rec"), lax.axis_index("attr")
    n_rec, n_attr = lax.axis_size("rec"), lax.axis_size("attr")
    n_x = n_attr // 2
    half, x = lax.rem(attr, 2), lax.div(attr, 2)
    h1 = buf.shape[0] // 2
    h2 = h1 // n_x
    base = half * h1 + x * h2
    greet(peers_of(("attr",)) + peers_of(("rec",)))
    sem = iter(range(1000))

    def push(src, dst, device):
        k = next(sem)
        copy = pltpu.make_async_remote_copy(
            src_ref=src, dst_ref=dst, send_sem=sems.at[0, k], recv_sem=sems.at[1, k],
            device_id=device, device_id_type=MESH,
        )
        copy.start()
        return copy

    def settle(copies):
        for copy in copies:
            copy.wait()

    partner = {"attr": x * 2 + 1 - half}
    columns = [lax.rem(x + d, n_x) for d in range(1, n_x)]
    lines = [lax.rem(rec + d, n_rec) for d in range(1, n_rec)]
    first = [push(buf.at[pl.ds((1 - half) * h1, h1)], r1, partner)]
    swaps = start_swap(("attr",), cells, cells_out, c_send, c_recv)
    settle(first)
    for b in range(h1):
        s1[b] = (buf[half * h1 + b].astype(F32) + r1[b].astype(F32)).astype(BF16)
    settle([
        push(s1.at[pl.ds(c * h2, h2)], r2.at[d], {"attr": c * 2 + half}) for d, c in enumerate(columns)
    ])
    for b in range(h2):
        value = s1[x * h2 + b].astype(F32)
        for d in range(n_x - 1):
            value += r2[d, b].astype(F32)
        s2[b] = value.astype(BF16)
    settle([push(s2.at[:, r], r3.at[d], {"rec": r}) for d, r in enumerate(lines)])
    for b in range(h2):
        value = s2[b, rec].astype(F32)
        for d in range(n_rec - 1):
            value += r3[d, b].astype(F32)
        out[base + b, rec] = value.astype(BF16)
    own = out.at[pl.ds(base, h2), rec]
    settle([push(own, own, {"rec": r}) for r in lines])
    own = out.at[pl.ds(base, h2)]
    settle([push(own, own, {"attr": c * 2 + half}) for c in columns])
    own = out.at[pl.ds(half * h1, h1)]
    settle([push(own, own, partner)])
    settle(swaps)


def local(
    cells, cotangent, qkv_attr, out_attr, qkv_samp, out_samp, up_weight, down_weight, train_split
):
    n_rec, n_attr = lax.axis_size("rec"), lax.axis_size("attr")
    rows, cols = cells.shape[0], cells.shape[1] // E
    tokens = rows * cols
    width = cols * n_attr
    length = rows * n_rec
    few = rows // n_attr
    thin = cols // n_rec
    n_a = tokens // width
    size = length * max(1, min(256 // length, thin))
    n_s = tokens // size

    def shape(*dims, dtype=BF16):
        return jax.ShapeDtypeStruct(dims, dtype)

    def call(kernel, outs, scratch, *args):
        return pl.pallas_call(
            kernel,
            out_shape=outs,
            in_specs=[VMEM] * len(args),
            out_specs=[VMEM] * len(outs),
            scratch_shapes=scratch,
            compiler_params=pltpu.CompilerParams(vmem_limit_bytes=48 * 2**20),
        )(*args)

    flat = [pltpu.VMEM((tokens, E), F32)]
    table = shape(tokens, E)
    acc = pltpu.VMEM((3, tokens, E), F32)
    tall = pltpu.VMEM((tokens, E), BF16)

    c_send, g_send = call(
        unpack_kernel, [table, table], flat, cells, cotangent, place((cols, rows), (1, 0))
    )
    c_got, g_got = swap(
        (("attr",), ("rec",)),
        [c_send.reshape(n_attr, -1, E), g_send.reshape(n_rec, -1, E)],
        0,
    )
    spread = place((few, n_attr, n_rec, thin), (2, 1, 0, 3))
    gathered = place((n_rec, n_attr, few, thin), (2, 1, 0, 3))
    f_send, x_attr, mixed_attr, qkv_kept, p_kept = call(
        functools.partial(attr_kernel, n_a, width),
        [table, table, table, shape(3, tokens, E), shape(n_a, HEADS, width, width, dtype=F32)],
        [acc],
        c_got.reshape(tokens, E), place((n_attr, few, cols), (1, 0, 2)), spread, qkv_attr, out_attr,
    )
    split = (n_rec, n_attr, few * thin, E)
    (f_got,) = swap((("rec", "attr"),), [f_send.reshape(split)], 1)
    back, grads_middle = call(
        functools.partial(middle_kernel, n_s, size, length),
        [table, shape(12, E, E)],
        [
            tall, tall, pltpu.VMEM((3, tokens, E), BF16), pltpu.VMEM((n_s, HEADS, size, size), F32),
            acc, tall, pltpu.VMEM((tokens, E), F32), pltpu.VMEM((size, size), F32),
        ],
        f_got.reshape(tokens, E), g_got.reshape(tokens, E),
        place((length, thin), (1, 0)),
        place((n_rec, thin, rows), (1, 0, 2)),
        place((thin, length), (1, 0)),
        jnp.tile(train_split, size // length)[None, :],
        qkv_samp, out_samp, up_weight, down_weight,
    )
    (b_got,) = swap((("rec", "attr"),), [back.reshape(split)], 2)
    last, grads_attr = call(
        functools.partial(attr_back_kernel, n_a, width),
        [table, shape(4, E, E)],
        [acc, tall],
        b_got.reshape(tokens, E), gathered, x_attr, mixed_attr, qkv_kept, p_kept, qkv_attr, out_attr,
    )
    last = moved_out(last, few, n_attr, cols)
    grads = jnp.concatenate([grads_middle, grads_attr], axis=0)
    part = E // n_rec
    h1 = BLOCKS // 2
    h2 = h1 // (n_attr // 2)
    o_got, totals = pl.pallas_call(
        total_kernel,
        out_shape=[shape(n_attr, few, cols, E), shape(BLOCKS, n_rec, part, E)],
        in_specs=[VMEM] * 2,
        out_specs=[VMEM] * 2,
        scratch_shapes=[
            pltpu.VMEM((h1, n_rec, part, E), BF16),
            pltpu.VMEM((max(1, n_attr // 2 - 1), h2, n_rec, part, E), BF16),
            pltpu.VMEM((max(1, n_rec - 1), h2, part, E), BF16),
            pltpu.VMEM((h1, n_rec, part, E), BF16),
            pltpu.VMEM((h2, n_rec, part, E), BF16),
            pltpu.SemaphoreType.DMA((n_attr,)),
            pltpu.SemaphoreType.DMA((n_attr,)),
            pltpu.SemaphoreType.DMA((2, 2 * (n_rec + n_attr // 2))),
        ],
        compiler_params=pltpu.CompilerParams(collective_id=3, has_side_effects=True),
    )(last, grads.reshape(BLOCKS, n_rec, part, E))
    factor = 1.0 / math.sqrt(length * width)
    out = call(
        functools.partial(finish_kernel, factor),
        [
            shape(rows, cols * E), shape(E, 3 * E, dtype=F32), shape(E, E, dtype=F32),
            shape(E, 3 * E, dtype=F32), shape(E, E, dtype=F32),
            shape(E, 4 * E, dtype=F32), shape(4 * E, E, dtype=F32),
        ],
        flat,
        o_got.reshape(tokens, E), place((rows, cols), (1, 0)), totals.reshape(BLOCKS, E, E),
    )
    return tuple(out)


def moved_out(last, few, n_attr, cols):
    return last.reshape(few, n_attr, cols, E).swapaxes(0, 1)


def solution(mesh):
    both = P(("groups", "rec"), "attr")
    in_specs = (both, both, P(), P(), P(), P(), P(), P(), P("groups"))
    out_specs = (both,) + (P("groups", None),) * 6
    return jax.shard_map(local, mesh=mesh, in_specs=in_specs, out_specs=out_specs, check_vma=False)
```

profile of v0, /device:TPU:0, one launch (start us, length us, event | category | flops | bytes accessed | tf_op | source)
XLA Modules:
  0.0 149.9 jit_solution(7694295643306513623)
XLA Ops:
  0.6 0.0 copy-start.28
  0.6 0.0 copy-start.29
  0.7 0.7 tile.2
  1.3 0.1 broadcast_in_dim_tile.3.split
  1.4 1.1 copy.26.down
  2.5 0.0 copy-start.24
  2.5 0.9 copy-done.24
  3.5 0.0 copy-start.25
  3.5 0.9 copy-done.25
  4.4 0.0 copy-start.33
  4.4 0.7 copy-done.33
  5.1 0.4 shard_map.216
  5.5 0.0 copy-start.19
  5.5 0.7 copy-done.19
  6.2 0.0 copy-start.20
  6.2 0.7 copy-done.20
  6.9 13.4 %shard_map.217 = (bf16[4,128,192]{2,1,0:T(8,128)(2,1)}, bf16[4,128,192]{2,1,0:T(8,128)(2,1)}) custom-call(bf16[4,128,192]{2,1,0:T(8,128)(2,1)} %bitcast.22, bf16[4,128,192]{2,1,0:T(8,128)(2,1)} %bitcast.23), custom_call_target="tpu_custom_call" | custom-call | tf_op jit(solution)/shard_map/pallas_call | solution.py:263
  20.3 0.0 copy-start.5
  20.3 0.9 copy-done.5
  21.2 0.0 copy-start.9
  21.2 0.9 copy-done.9
  22.1 0.9 copy-done.16
  23.1 0.7 copy-done.31
  23.8 0.7 copy-done.32
  24.4 7.2 %shard_map.218 = (bf16[512,192]{1,0:T(8,128)(2,1)S(1)}, bf16[512,192]{1,0:T(8,128)(2,1)S(1)}, bf16[512,192]{1,0:T(8,128)(2,1)S(1)}, bf16[3,512,192]{2,1,0:T(8,128)(2,1)S(1)}, f32[2,6,256,256]{3,2,1,0:T(8,128)S(1)}) custom-call(bf16[512,192]{1,0:T(8,128)(2,1)S(1)} %bitcast.18, s32[1,512]{1,0:T(1,128)S(1)} %copy-done.31, s32[1,512]{1,0:T(1,128)S(1)} %copy-done.32, ...), custom_call_target="tpu_custom_call" | custom-call | tf_op jit(solution)/shard_map/pallas_call | solution.py:346
  31.7 0.0 copy-start.7
  31.7 0.9 copy-done.7
  32.6 0.7 copy-done.12
  33.3 0.7 copy-done.14
  34.0 0.7 copy-done.18
  34.7 11.5 %shard_map.219 = bf16[4,4,32,192]{3,2,1,0:T(8,128)(2,1)} custom-call(bf16[4,4,32,192]{3,2,1,0:T(8,128)(2,1)} %bitcast.20), custom_call_target="tpu_custom_call" | custom-call | tf_op jit(solution)/shard_map/pallas_call | solution.py:263
  46.1 0.0 copy-done.28
  46.2 0.0 copy-done.29
  46.2 0.0 copy-start.4
  46.2 0.9 copy-done.4
  47.1 1.0 copy-done.11
  48.1 0.9 copy-done.21
  49.0 0.9 copy-done.23
  50.0 0.9 copy-done.26
  50.9 0.7 copy-done.30
  51.5 16.7 %shard_map.220 = (bf16[512,192]{1,0:T(8,128)(2,1)S(1)}, bf16[12,192,192]{2,1,0:T(8,128)(2,1)S(1)}) custom-call(bf16[512,192]{1,0:T(8,128)(2,1)S(1)} %bitcast.17, bf16[512,192]{1,0:T(8,128)(2,1)S(1)} %bitcast.24, s32[1,512]{1,0:T(1,128)S(1)} %copy-done.30, s32[1,512]{1,0:T(1,128)S(1)} %copy-done.29, s32[1,512]{1,0:T(1,128)S(1)} %copy-done.28, ...), custom_call_target="tpu_custom_call" | custom-call | tf_op jit(solution)/shard_map/pallas_call | solution.py:346
  68.2 0.0 copy-start.1
  68.2 1.0 copy-done.1
  69.3 0.7 copy-done.17
  70.0 11.9 %shard_map.221 = bf16[4,4,32,192]{3,2,1,0:T(8,128)(2,1)} custom-call(bf16[4,4,32,192]{3,2,1,0:T(8,128)(2,1)} %bitcast.19), custom_call_target="tpu_custom_call" | custom-call | tf_op jit(solution)/shard_map/pallas_call | solution.py:263
  81.9 0.0 copy-done.27
  81.9 0.0 copy-start.3
  81.9 0.9 copy-done.3
  82.8 0.9 copy-done.6
  83.8 1.1 copy-done.8
  84.9 0.9 copy-done.10
  85.8 0.9 copy-done.13
  86.8 0.9 copy-done.15
  87.7 7.3 %shard_map.222 = (bf16[512,192]{1,0:T(8,128)(2,1)S(1)}, bf16[4,192,192]{2,1,0:T(8,128)(2,1)S(1)}) custom-call(bf16[512,192]{1,0:T(8,128)(2,1)S(1)} %bitcast.16, s32[1,512]{1,0:T(1,128)S(1)} %copy-done.27, bf16[512,192]{1,0:T(8,128)(2,1)S(1)} %copy-done.13, bf16[512,192]{1,0:T(8,128)(2,1)S(1)} %copy-done.15, bf16[3,512,192]{2,1,0:T(8,128)(2,1)S(1)} %copy-done.8, ...), custom_call_target="tpu_custom_call" | custom-call | tf_op jit(solution)/shard_map/pallas_call | solution.py:346
  95.1 0.7 copy.30
  95.8 0.0 copy-done.2
  95.8 1.4 pad_maximum_fusion
  97.2 47.5 %shard_map.223 = (bf16[4,2,64,192]{3,2,1,0:T(8,128)(2,1)}, bf16[16,4,48,192]{3,2,1,0:T(8,128)(2,1)}) custom-call(bf16[4,2,64,192]{3,2,1,0:T(8,128)(2,1)} %bitcast.27, bf16[16,4,48,192]{3,2,1,0:T(8,128)(2,1)} %bitcast.26), custom_call_target="tpu_custom_call" | custom-call | tf_op jit(solution)/shard_map/pallas_call | solution.py:404
  144.8 0.0 copy-done.34
  144.8 0.0 copy-start
  144.8 1.4 copy-done
  146.2 0.9 copy-done.22
  147.1 1.7 %shard_map.224 = (bf16[8,12288]{1,0:T(8,128)(2,1)}, f32[192,576]{1,0:T(8,128)}, f32[192,192]{1,0:T(8,128)}, f32[192,576]{1,0:T(8,128)}, f32[192,192]{1,0:T(8,128...) custom-call(bf16[512,192]{1,0:T(8,128)(2,1)S(1)} %bitcast.25, s32[1,512]{1,0:T(1,128)S(1)} %copy-done.34, ...), custom_call_target="tpu_custom_call" | custom-call | tf_op jit(solution)/shard_map/pallas_call | solution.py:346
  148.8 1.1 copy.28
  (21 shorter events, 0.0 us)
Async XLA Ops:
  0.6 45.5 %copy-start.28 = (s32[1,512]{1,0:T(1,128)S(1)}, s32[1,512]{1,0:T(1,128)}, u32[]{:S(2)}) copy-start(s32[1,512]{1,0:T(1,128)} %constant.22.clone.where_back) | copy-start | bytes 6148
  0.6 45.5 %copy-start.29 = (s32[1,512]{1,0:T(1,128)S(1)}, s32[1,512]{1,0:T(1,128)}, u32[]{:S(2)}) copy-start(s32[1,512]{1,0:T(1,128)} %constant.21.clone.where_g) | copy-start | bytes 6148
  2.5 0.9 copy-start.24
  3.5 0.9 copy-start.25
  4.4 0.7 copy-start.33
  5.5 0.7 copy-start.19
  6.2 0.7 copy-start.20
  20.3 0.9 copy-start.5
  21.2 0.9 copy-start.9
  22.1 0.9 copy-start.16
  23.1 0.7 copy-start.31
  23.8 0.7 copy-start.32
  24.4 57.4 %copy-start.27 = (s32[1,512]{1,0:T(1,128)S(1)}, s32[1,512]{1,0:T(1,128)}, u32[]{:S(2)}) copy-start(s32[1,512]{1,0:T(1,128)} %constant.18.clone.where) | copy-start | bytes 6148
  31.7 0.9 copy-start.7
  32.6 0.7 copy-start.12
  33.3 0.7 copy-start.14
  34.0 0.7 copy-start.18
  46.2 1.0 copy-start.4
  47.1 1.0 copy-start.11
  48.1 0.9 copy-start.21
  49.0 0.9 copy-start.23
  50.0 0.9 copy-start.26
  50.9 0.7 copy-start.30
  68.2 1.0 copy-start.1
  69.3 0.7 copy-start.17
  81.9 1.0 copy-start.3
  82.8 0.9 copy-start.6
  83.8 1.1 copy-start.8
  84.9 0.9 copy-start.10
  85.8 0.9 copy-start.13
  86.8 0.9 copy-start.15
  87.7 8.1 %copy-start.2 = (bf16[12,192,192]{2,1,0:T(8,128)(2,1)S(1)}, bf16[12,192,192]{2,1,0:T(8,128)(2,1)}, u32[]{:S(2)}) copy-start(bf16[12,192,192]{2,1,0:T(8,128)(2,1)} %copy-done.1) | copy-start | bytes 2654212
  97.2 47.5 %copy-start.34 = (s32[1,512]{1,0:T(1,128)S(1)}, s32[1,512]{1,0:T(1,128)}, u32[]{:S(2)}) copy-start(s32[1,512]{1,0:T(1,128)} %constant.23.clone.where) | copy-start | bytes 6148
  144.8 1.4 copy-start
  146.2 0.9 copy-start.22
where the time goes:
time: 152 us; the launch traced here: 150 us
  Pallas kernels  118 us (78%)
  local copies, waits for them, and re-layouts  30 us (20%)
    pallas_call x1, Pallas kernels, local(): pl.pallas_call(total_kernel, out_shape=[shape(n_attr, few, cols, E), shap...  47.5 us
    pallas_call x3, Pallas kernels, swap(): pl.pallas_call(functools.partial(swap_kernel, flows), out_shape=[jax.Shap...  36.7 us
    pallas_call x5, Pallas kernels, call(): pl.pallas_call(kernel, out_shape=outs, in_specs=[VMEM] * len(args), out_s...  33.4 us
    unnamed x71, local copies, waits for them, and re-layouts  27.5 us

commit v1 on v0

v1 whole, which is shorter than its diff:
```python
import functools
import math

import jax
import jax.numpy as jnp
import numpy as np
from jax import lax
from jax.experimental import pallas as pl
from jax.experimental.pallas import tpu as pltpu
from jax.sharding import PartitionSpec as P

E = 192
HEADS = 6
HD = E // HEADS
SCALE = 1.0 / math.sqrt(HD)
BLOCKS = 16
F32 = jnp.float32
BF16 = jnp.bfloat16
MESH = pl.DeviceIdType.MESH
NN = (((1,), (0,)), ((), ()))
NT = (((1,), (1,)), ((), ()))
TN = (((0,), (0,)), ((), ()))
VMEM = pl.BlockSpec(memory_space=pltpu.VMEM)
ANY = pl.BlockSpec(memory_space=pl.ANY)


def dot(a, b, form=NN):
    return lax.dot_general(a, b, form, preferred_element_type=F32)


def place(sizes, order):
    index = np.arange(math.prod(sizes)).reshape(sizes).transpose(order).reshape(-1)
    there = np.empty_like(index)
    there[index] = np.arange(index.size)
    return there.astype(np.int32)


def moved(where_ref, x):
    n = x.shape[0]
    hot = lax.broadcasted_iota(jnp.int32, (n, n), 0) == where_ref[...]
    return dot(jnp.where(hot, 1.0, 0.0).astype(BF16), x)


def put(ref, b, value):
    pieces, part = ref.shape[1], ref.shape[2]
    side = jnp.concatenate([value[: E // 2], value[E // 2:]], axis=1)
    for r in range(pieces):
        ref[b, r] = side[r * part:(r + 1) * part].astype(BF16)


def pack(ref, value, few):
    run = value.shape[0] // few
    pieces, part = ref.shape[0], ref.shape[1]
    side = jnp.concatenate([value[k * run:(k + 1) * run] for k in range(few)], axis=1)
    for r in range(pieces):
        ref[r] = side[r * part:(r + 1) * part].astype(BF16)


def unpack(ref, flat, few):
    pieces, part = ref.shape[0], ref.shape[1]
    run = pieces * part
    for r in range(pieces):
        side = ref[r].astype(F32)
        for k in range(few):
            flat[k * run + r * part:k * run + (r + 1) * part] = side[:, k * E:(k + 1) * E]
    return flat[...].astype(BF16)


def norm(x):
    center = x - jnp.mean(x, axis=-1, keepdims=True)
    scale = lax.rsqrt(jnp.mean(center * center, axis=-1, keepdims=True) + 1e-05)
    return center * scale, scale


def norm_back(hat, scale, grad):
    return scale * (
        grad
        - jnp.mean(grad, axis=-1, keepdims=True)
        - hat * jnp.mean(grad * hat, axis=-1, keepdims=True)
    )


def head_mask(h):
    lane = lax.broadcasted_iota(jnp.int32, (1, E), 1)
    return jnp.where((lane >= h * HD) & (lane < (h + 1) * HD), 1.0, 0.0).astype(F32)


def attend(x_ref, qkv, out, qkv_s, p_s, acc, n, size, bias):
    normed = norm(x_ref[...].astype(F32))[0].astype(BF16)
    for t in range(3):
        qkv_s[t] = dot(normed, qkv[:, t * E:(t + 1) * E]).astype(BF16)
    acc[0] = jnp.zeros(acc.shape[1:], F32)

    def head(h, _):
        mask = head_mask(h)
        for b in range(n):
            rows = pl.ds(b * size, size)
            s = dot(qkv_s[0, rows] * mask.astype(BF16), qkv_s[1, rows], NT) * SCALE
            if bias is not None:
                s = jnp.where(bias[...] > 0, s, -1e30)
            e = jnp.exp(s - jnp.max(s, axis=-1, keepdims=True))
            p = e * (1.0 / jnp.sum(e, axis=-1, keepdims=True))
            p_s[b, h] = p
            acc[0, rows] += dot(p.astype(BF16), qkv_s[2, rows]) * mask
        return 0

    lax.fori_loop(0, HEADS, head, 0)
    mixed = acc[0].astype(BF16)
    return normed, mixed, (x_ref[...].astype(F32) + dot(mixed, out)).astype(BF16)


def attend_back(x, g, mixed, qkv, out, qkv_s, p_s, acc, dm_s, grads, first, n, size):
    dm_s[...] = dot(g, out, NT).astype(BF16)
    put(grads, first + 3, dot(mixed, g, TN))
    acc[...] = jnp.zeros(acc.shape, F32)

    def head(h, _):
        mask = head_mask(h)
        for b in range(n):
            rows = pl.ds(b * size, size)
            dm = dm_s[rows] * mask.astype(BF16)
            p = p_s[b, h]
            dp = dot(dm, qkv_s[2, rows], NT).astype(BF16).astype(F32)
            ds = (p * (dp - jnp.sum(dp * p, axis=-1, keepdims=True)) * SCALE).astype(BF16)
            acc[0, rows] += dot(ds, qkv_s[1, rows]) * mask
            acc[1, rows] += dot(ds, qkv_s[0, rows], TN) * mask
            acc[2, rows] += dot(p.astype(BF16), dm, TN)
        return 0

    lax.fori_loop(0, HEADS, head, 0)
    hat, scale = norm(x.astype(F32))
    normed = hat.astype(BF16)
    dn = None
    for t in range(3):
        d = acc[t].astype(BF16)
        put(grads, first + t, dot(normed, d, TN))
        part = dot(d, qkv[:, t * E:(t + 1) * E], NT)
        dn = part if dn is None else dn + part
    return (g.astype(F32) + norm_back(hat, scale, dn.astype(BF16).astype(F32))).astype(BF16)


def rows_of(cells, flat):
    rows = cells.shape[0]
    for a in range(cells.shape[1] // E):
        flat[a * rows:(a + 1) * rows] = cells[:, a * E:(a + 1) * E].astype(F32)
    return flat[...].astype(BF16)


def shifts_of(axes):
    sizes = [lax.axis_size(a) for a in axes]
    return [s for s in np.ndindex(*sizes) if any(s)], sizes


def peers_of(axes):
    shifts, sizes = shifts_of(axes)
    me = [lax.axis_index(a) for a in axes]
    return [[lax.rem(m + d, n) for m, d, n in zip(me, s, sizes)] for s in shifts]


def start_swap(axes, src, dst, sems):
    _, sizes = shifts_of(axes)

    def flat(where):
        number = where[0]
        for w, n in zip(where[1:], sizes[1:]):
            number = number * n + w
        return number

    me = flat([lax.axis_index(a) for a in axes])
    copies = []
    for k, to in enumerate(peers_of(axes)):
        copy = pltpu.make_async_remote_copy(
            src_ref=src.at[flat(to)],
            dst_ref=dst.at[me],
            send_sem=sems.at[0, k],
            recv_sem=sems.at[1, k],
            device_id=dict(zip(axes, to)),
            device_id_type=MESH,
        )
        copy.start()
        copies.append(copy)
    dst[me] = src[me]
    return copies


def settle(copies):
    for copy in copies:
        copy.wait()


def total_steps(buf, out, first, count, r1, r2, r3, s1, s2, sems):
    rec, attr = lax.axis_index("rec"), lax.axis_index("attr")
    n_rec, n_x = lax.axis_size("rec"), lax.axis_size("attr") // 2
    half, x = lax.rem(attr, 2), lax.div(attr, 2)
    h1 = count // 2
    h2 = h1 // n_x
    base = first + half * h1 + x * h2
    sem = iter(range(sems.shape[1]))

    def push(src, dst, device):
        k = next(sem)
        copy = pltpu.make_async_remote_copy(
            src_ref=src, dst_ref=dst, send_sem=sems.at[0, k], recv_sem=sems.at[1, k],
            device_id=device, device_id_type=MESH,
        )
        copy.start()
        return copy

    partner = {"attr": x * 2 + 1 - half}
    columns = [lax.rem(x + d, n_x) for d in range(1, n_x)]
    lines = [lax.rem(rec + d, n_rec) for d in range(1, n_rec)]
    copies = [push(buf.at[pl.ds(first + (1 - half) * h1, h1)], r1, partner)]
    yield
    settle(copies)
    for b in range(h1):
        s1[b] = (buf[first + half * h1 + b].astype(F32) + r1[b].astype(F32)).astype(BF16)
    copies = [
        push(s1.at[pl.ds(c * h2, h2)], r2.at[d], {"attr": c * 2 + half}) for d, c in enumerate(columns)
    ]
    yield
    settle(copies)
    for b in range(h2):
        value = s1[x * h2 + b].astype(F32)
        for d in range(n_x - 1):
            value += r2[d, b].astype(F32)
        s2[b] = value.astype(BF16)
    copies = [push(s2.at[:, r], r3.at[d], {"rec": r}) for d, r in enumerate(lines)]
    yield
    settle(copies)
    for b in range(h2):
        value = s2[b, rec].astype(F32)
        for d in range(n_rec - 1):
            value += r3[d, b].astype(F32)
        out[base + b, rec] = value.astype(BF16)
    own = out.at[pl.ds(base, h2), rec]
    copies = [push(own, own, {"rec": r}) for r in lines]
    yield
    settle(copies)
    own = out.at[pl.ds(base, h2)]
    copies = [push(own, own, {"attr": c * 2 + half}) for c in columns]
    yield
    settle(copies)
    own = out.at[pl.ds(first + half * h1, h1)]
    copies = [push(own, own, partner)]
    yield
    settle(copies)
    yield


COUNTS = (8, 4, 4)


def layer_kernel(
    size_a, size_s, length, few,
    cells_h, cot_h, qkva_h, outa_h, qkvs_h, outs_h, up_h, down_h, split_h, place_h,
    o_got, totals,
    cells, cot, qkva, outa, qkvs, outs, up, down, split, places, in_sems,
    flat, c_send, c_got, g_send, g_got, f_send, f_got, b_send, b_got, o_send,
    x_a, mixed_a, qkv_a, p_a, x_s, g_s, qkv_s, p_s, acc, dm_s, dn_s, bias, grads,
    c_sems, g_sems, f_sems, b_sems, o_sems, *sums,
):
    tokens = flat.shape[0]
    n_a, n_s = tokens // size_a, tokens // size_s
    loads = {}
    pairs = (
        (cells_h, cells), (place_h, places), (cot_h, cot), (qkva_h, qkva), (outa_h, outa),
        (split_h, split), (qkvs_h, qkvs), (outs_h, outs), (up_h, up), (down_h, down),
    )
    for k, (src, dst) in enumerate(pairs):
        loads[k] = pltpu.make_async_copy(src, dst, in_sems.at[k])
        loads[k].start()
    barrier = pltpu.get_barrier_semaphore()
    peers = peers_of(("rec", "attr"))
    for r, a in peers:
        pl.semaphore_signal(barrier, inc=1, device_id={"rec": r, "attr": a}, device_id_type=MESH)

    def at(k):
        return places.at[k:k + 1]

    loads[0].wait()
    loads[1].wait()
    pack(c_send, moved(at(0), rows_of(cells, flat)), few)
    pl.semaphore_wait(barrier, len(peers))
    c_copies = start_swap(("attr",), c_send, c_got, c_sems)
    loads[2].wait()
    pack(g_send, moved(at(1), rows_of(cot, flat)), few)
    g_copies = start_swap(("rec",), g_send, g_got, g_sems)
    for k in range(3, len(pairs)):
        loads[k].wait()
    settle(c_copies)
    x_a[...] = unpack(c_got, flat, few)
    _, mixed, first = attend(x_a, qkva, outa[...], qkv_a, p_a, acc, n_a, size_a, None)
    mixed_a[...] = mixed
    pack(f_send, moved(at(2), first), few)
    f_copies = start_swap(("rec", "attr"), f_send, f_got, f_sems)

    row = lax.broadcasted_iota(jnp.int32, (size_s, size_s), 0)
    column = lax.broadcasted_iota(jnp.int32, (size_s, size_s), 1)
    same = None
    for s in range(size_s // length):
        low, high = s * length, (s + 1) * length
        inside = (row >= low) & (row < high) & (column >= low) & (column < high)
        same = inside if same is None else same | inside
    bias[...] = jnp.where(same, split[...].astype(F32), 0.0)
    settle(g_copies)
    g_s[...] = moved(at(4), unpack(g_got, flat, few)).astype(BF16)
    settle(f_copies)
    x_s[...] = moved(at(3), unpack(f_got, flat, few)).astype(BF16)
    _, mixed, second = attend(x_s, qkvs, outs[...], qkv_s, p_s, acc, n_s, size_s, bias)
    hat, scale = norm(second.astype(F32))
    normed = hat.astype(BF16)
    g = g_s[...]
    for c in range(up.shape[1] // E):
        w_up = up[:, c * E:(c + 1) * E]
        pre = dot(normed, w_up)
        cdf = 0.5 * (1.0 + lax.erf(pre * (1.0 / math.sqrt(2.0))))
        hidden = (pre * cdf).astype(BF16)
        slope = cdf + pre * (jnp.exp(pre * pre * -0.5) * (1.0 / math.sqrt(2.0 * math.pi)))
        dh = dot(g, down[c * E:(c + 1) * E], NT).astype(BF16).astype(F32)
        dpre = (dh * slope).astype(BF16)
        put(grads, c, dot(normed, dpre, TN))
        put(grads, 4 + c, dot(hidden, g, TN))
        part = dot(dpre, w_up, NT)
        if c == 0:
            dn_s[...] = part
        else:
            dn_s[...] += part
    starts = (0, COUNTS[0], COUNTS[0] + COUNTS[1])
    ffn, samp, attr = (
        total_steps(grads, totals, starts[k], COUNTS[k], *sums[6 * k:6 * k + 6]) for k in range(3)
    )
    next(ffn)
    dn = dn_s[...].astype(BF16).astype(F32)
    g = (g.astype(F32) + norm_back(hat, scale, dn)).astype(BF16)
    back = attend_back(
        x_s[...], g, mixed, qkvs, outs[...], qkv_s, p_s, acc, dm_s, grads, starts[1], n_s, size_s
    )
    pack(b_send, moved(at(5), back), few)
    b_copies = start_swap(("rec", "attr"), b_send, b_got, b_sems)
    next(samp)
    next(ffn)
    settle(b_copies)
    next(samp)
    next(ffn)
    g = moved(at(6), unpack(b_got, flat, few)).astype(BF16)
    back = attend_back(
        x_a[...], g, mixed_a[...], qkva, outa[...], qkv_a, p_a, acc, dm_s, grads, starts[2], n_a, size_a
    )
    pack(o_send, back.astype(F32), few)
    o_copies = start_swap(("attr",), o_send, o_got, o_sems)
    next(attr)
    for steps in (ffn, samp, attr, ffn, samp, attr, ffn, samp, attr, ffn, samp, attr, samp, attr, attr):
        next(steps)
    settle(o_copies)


def finish_kernel(
    factor, few, tokens_h, places_h, total_h, cells, qa, oa, qs, os, gu, gd,
    tokens, places, total, sems, flat, out_flat, tmp,
):
    loads = [
        pltpu.make_async_copy(src, dst, sems.at[k])
        for k, (src, dst) in enumerate(((tokens_h, tokens), (places_h, places), (total_h, total)))
    ]
    for load in loads:
        load.start()
    rows = cells.shape[0]
    loads[0].wait()
    loads[1].wait()
    out_flat[...] = moved(places.at[7:8], unpack(tokens, flat, few))
    for a in range(0, cells.shape[1] // E, 2):
        pair = [out_flat[(a + k) * rows:(a + k + 1) * rows] for k in range(2)]
        cells[:, a * E:(a + 2) * E] = jnp.concatenate(pair, axis=1).astype(BF16)
    loads[2].wait()

    def block(b):
        part = total.shape[2]
        for r in range(total.shape[1]):
            tmp[b, r * part:(r + 1) * part] = total[b, r].astype(F32) * factor
        side = tmp[b]
        return jnp.concatenate([side[:, :E], side[:, E:]], axis=0)

    gu[...] = jnp.concatenate([block(c) for c in range(4)], axis=1)
    for c in range(4):
        gd[c * E:(c + 1) * E] = block(4 + c)
    for ref, start in ((qs, 8), (qa, 12)):
        ref[...] = jnp.concatenate([block(start + t) for t in range(3)], axis=1)
    os[...] = block(11)
    oa[...] = block(15)


def local(
    cells, cotangent, qkv_attr, out_attr, qkv_samp, out_samp, up_weight, down_weight, train_split
):
    n_rec, n_attr = lax.axis_size("rec"), lax.axis_size("attr")
    rows, cols = cells.shape[0], cells.shape[1] // E
    tokens = rows * cols
    width = cols * n_attr
    length = rows * n_rec
    few = rows // n_attr
    thin = cols // n_rec
    size = length * max(1, min(256 // length, thin))
    places = jnp.asarray(np.stack([
        place((cols, n_attr, few), (2, 1, 0)),
        place((n_rec, thin, n_attr, few), (3, 0, 1, 2)),
        place((few, n_attr, n_rec, thin), (0, 2, 1, 3)),
        place((few, n_rec, n_attr, thin), (3, 1, 2, 0)),
        place((few, n_rec, thin, n_attr), (2, 1, 3, 0)),
        place((thin, n_rec, n_attr, few), (3, 1, 2, 0)),
        place((few, n_rec, n_attr, thin), (0, 2, 1, 3)),
        place((few, n_attr, cols), (2, 1, 0)),
    ]))
    split = jnp.tile(train_split, size // length)[None, :]
    all_devices = n_rec * n_attr
    part = E // 2 // n_rec
    n_x = n_attr // 2

    def shape(*dims, dtype=BF16):
        return jax.ShapeDtypeStruct(dims, dtype)

    def vmem(*dims, dtype=BF16):
        return pltpu.VMEM(dims, dtype)

    args = (
        cells, cotangent, qkv_attr, out_attr, qkv_samp, out_samp, up_weight, down_weight, split, places
    )
    c_buf = vmem(n_attr, cols, few * E)
    g_buf = vmem(n_rec, thin * n_attr, few * E)
    f_buf = vmem(all_devices, thin, few * E)
    table = vmem(tokens, E)
    sums = []
    for count in COUNTS:
        h1 = count // 2
        h2 = h1 // n_x
        sums += [
            vmem(h1, n_rec, part, 2 * E), vmem(max(1, n_x - 1), h2, n_rec, part, 2 * E),
            vmem(max(1, n_rec - 1), h2, part, 2 * E), vmem(h1, n_rec, part, 2 * E),
            vmem(h2, n_rec, part, 2 * E),
            pltpu.SemaphoreType.DMA((2, 2 * (n_rec + n_x - 1))),
        ]
    o_got, totals = pl.pallas_call(
        functools.partial(layer_kernel, width, size, length, few),
        out_shape=[shape(n_attr, cols, few * E), shape(BLOCKS, n_rec, part, 2 * E)],
        in_specs=[ANY] * len(args),
        out_specs=[VMEM] * 2,
        scratch_shapes=[pltpu.VMEM(a.shape, a.dtype) for a in args]
        + [
            pltpu.SemaphoreType.DMA((len(args),)),
            vmem(tokens, E, dtype=F32), c_buf, c_buf, g_buf, g_buf, f_buf, f_buf, f_buf, f_buf, c_buf,
            table, table, vmem(3, tokens, E), vmem(tokens // width, HEADS, width, width, dtype=F32),
            table, table, vmem(3, tokens, E), vmem(tokens // size, HEADS, size, size, dtype=F32),
            vmem(3, tokens, E, dtype=F32), table, vmem(tokens, E, dtype=F32),
            vmem(size, size, dtype=F32), vmem(BLOCKS, n_rec, part, 2 * E),
        ]
        + [
            pltpu.SemaphoreType.DMA((2, n))
            for n in (n_attr, n_rec, all_devices, all_devices, n_attr)
        ]
        + sums,
        compiler_params=pltpu.CompilerParams(
            collective_id=0, has_side_effects=True, vmem_limit_bytes=48 * 2**20
        ),
    )(*args)
    outs = [
        shape(rows, cols * E), shape(E, 3 * E, dtype=F32), shape(E, E, dtype=F32),
        shape(E, 3 * E, dtype=F32), shape(E, E, dtype=F32),
        shape(E, 4 * E, dtype=F32), shape(4 * E, E, dtype=F32),
    ]
    last = (o_got, places, totals)
    out = pl.pallas_call(
        functools.partial(finish_kernel, 1.0 / math.sqrt(length * width), few),
        out_shape=outs,
        in_specs=[ANY] * 3,
        out_specs=[VMEM] * len(outs),
        scratch_shapes=[pltpu.VMEM(a.shape, a.dtype) for a in last]
        + [
            pltpu.SemaphoreType.DMA((3,)), vmem(tokens, E, dtype=F32), vmem(tokens, E, dtype=F32),
            vmem(BLOCKS, E // 2, 2 * E, dtype=F32),
        ],
        compiler_params=pltpu.CompilerParams(vmem_limit_bytes=48 * 2**20),
    )(*last)
    return tuple(out)


def solution(mesh):
    both = P(("groups", "rec"), "attr")
    in_specs = (both, both, P(), P(), P(), P(), P(), P(), P("groups"))
    out_specs = (both,) + (P("groups", None),) * 6
    return jax.shard_map(local, mesh=mesh, in_specs=in_specs, out_specs=out_specs, check_vma=False)
```

time: 152 us -> 91.5 us (0.60); the launches traced: 150 us -> 91.1 us
  Pallas kernels: 118 us -> 80.3 us
  local copies, waits for them, and re-layouts: 30 us -> 10.1 us
    pallas_call x9 -> x2, Pallas kernels: 118 us -> 80.3 us  [the longest x1 77.4 us: local(): pl.pallas_call(functools.partial(layer_kernel, width, size, length, few),...]
    unnamed x71 -> x17, local copies, waits for them, and re-layouts: 27.5 us -> 8.33 us
where the time goes in v1:
time: 91.5 us; the launch traced here: 91.1 us
  Pallas kernels  80.3 us (88%)
  local copies, waits for them, and re-layouts  10.1 us (11%)
    pallas_call x1, Pallas kernels, local(): pl.pallas_call(functools.partial(layer_kernel, width, size, length, few),...  77.4 us
    unnamed x17, local copies, waits for them, and re-layouts  8.33 us
    pallas_call x1, Pallas kernels, local(): pl.pallas_call(functools.partial(finish_kernel, 1.0 / math.sqrt(length *...  2.86 us

profile of v1, /device:TPU:0, one launch (start us, length us, event | category | flops | bytes accessed | tf_op | source)
XLA Modules:
  0.0 91.1 jit_solution(308955274101334370)
XLA Ops:
  0.6 0.7 tile.2
  1.3 0.1 broadcast_in_dim_tile.3.split_h
  1.4 1.1 %copy.17.down_h = bf16[768,192]{1,0:T(8,128)(2,1)S(1)} copy(bf16[768,192]{0,1:T(8,128)(2,1)} %param.17) | data formatting | bytes 589824 | tf_op args[7]
  2.5 0.0 copy-start
  2.5 1.0 %copy-done = bf16[192,768]{1,0:T(8,128)(2,1)S(1)} copy-done((bf16[192,768]{1,0:T(8,128)(2,1)S(1)}, bf16[192,768]{1,0:T(8,128)(2,1)}, u32[]{:S(2)}) %copy-start) | copy-done | bytes 294936
  3.5 0.0 copy-start.1
  3.5 0.9 %copy-done.1 = bf16[192,576]{1,0:T(8,128)(2,1)S(1)} copy-done((bf16[192,576]{1,0:T(8,128)(2,1)S(1)}, bf16[192,576]{1,0:T(8,128)(2,1)}, u32[]{:S(2)}) %copy-start.1) | copy-done | bytes 221208
  4.4 0.0 copy-start.2
  4.4 0.9 %copy-done.2 = bf16[192,576]{1,0:T(8,128)(2,1)S(1)} copy-done((bf16[192,576]{1,0:T(8,128)(2,1)S(1)}, bf16[192,576]{1,0:T(8,128)(2,1)}, u32[]{:S(2)}) %copy-start.2) | copy-done | bytes 221208
  5.4 0.0 copy-start.3
  5.4 0.9 %copy-done.3 = bf16[8,12288]{1,0:T(8,128)(2,1)S(1)} copy-done((bf16[8,12288]{1,0:T(8,128)(2,1)S(1)}, bf16[8,12288]{1,0:T(8,128)(2,1)}, u32[]{:S(2)}) %copy-start.3) | copy-done | bytes 196632
  6.3 0.0 copy-start.4
  6.3 0.9 %copy-done.4 = bf16[8,12288]{1,0:T(8,128)(2,1)S(1)} copy-done((bf16[8,12288]{1,0:T(8,128)(2,1)S(1)}, bf16[8,12288]{1,0:T(8,128)(2,1)}, u32[]{:S(2)}) %copy-start.4) | copy-done | bytes 196632
  7.2 0.0 copy-start.5
  7.2 0.9 copy-done.5
  8.1 0.0 copy-start.6
  8.1 0.9 copy-done.6
  9.0 0.0 copy-start.7
  9.0 0.7 copy-done.7
  9.7 77.4 %shard_map.153 = (bf16[4,64,384]{2,1,0:T(8,128)(2,1)S(1)}, bf16[16,4,24,384]{3,2,1,0:T(8,128)(2,1)S(1)}) custom-call(bf16[8,12288]{1,0:T(8,128)(2,1)S(1)} %copy-done.3, bf16[8,12288]{1,0:T(8,128)(2,1)S(1)} %copy-done.4, bf16[192,576]{1,0:T(8,128)(2,1)S(1)} %copy-done.1, bf16[192,192]{1,0:T(8,128)(2,1)S(1)} %copy-done.5, bf16[192,576]{1,0:T(8,128)(2,1)S(1)} %copy-done.2, ...), custom_call_target="tpu_custom_call" | custom-call | tf_op jit(solution)/shard_map/pallas_call | solution.py:441
  87.1 2.9 %shard_map.154 = (bf16[8,12288]{1,0:T(8,128)(2,1)}, f32[192,576]{1,0:T(8,128)}, f32[192,192]{1,0:T(8,128)}, f32[192,576]{1,0:T(8,128)}, f32[192,192]{1,0:T(8,128...) custom-call(bf16[4,64,384]{2,1,0:T(8,128)(2,1)S(1)} %get-tuple-element.9.tokens_h, s32[8,512]{1,0:T(8,128)S(1)} %copy-done.7, ...), custom_call_target="tpu_custom_call" | custom-call | tf_op jit(solution)/shard_map/pallas_call | solution.py:470
  90.0 1.1 %copy.18 = f32[768,192]{0,1:T(8,128)} copy(f32[768,192]{1,0:T(8,128)S(1)} %get-tuple-element.17) | data formatting | bytes 1179648 | tf_op jit(solution)/shard_map/pallas_call | solution.py:470
Async XLA Ops:
  2.5 1.0 %copy-start = (bf16[192,768]{1,0:T(8,128)(2,1)S(1)}, bf16[192,768]{1,0:T(8,128)(2,1)}, u32[]{:S(2)}) copy-start(bf16[192,768]{1,0:T(8,128)(2,1)} %up_h.1) | copy-start | bytes 884740
  3.5 0.9 %copy-start.1 = (bf16[192,576]{1,0:T(8,128)(2,1)S(1)}, bf16[192,576]{1,0:T(8,128)(2,1)}, u32[]{:S(2)}) copy-start(bf16[192,576]{1,0:T(8,128)(2,1)} %qkva_h.1) | copy-start | bytes 663556
  4.4 0.9 %copy-start.2 = (bf16[192,576]{1,0:T(8,128)(2,1)S(1)}, bf16[192,576]{1,0:T(8,128)(2,1)}, u32[]{:S(2)}) copy-start(bf16[192,576]{1,0:T(8,128)(2,1)} %qkvs_h.1) | copy-start | bytes 663556
  5.4 0.9 %copy-start.3 = (bf16[8,12288]{1,0:T(8,128)(2,1)S(1)}, bf16[8,12288]{1,0:T(8,128)(2,1)}, u32[]{:S(2)}) copy-start(bf16[8,12288]{1,0:T(8,128)(2,1)} %cells_h.1) | copy-start | bytes 589828
  6.3 0.9 %copy-start.4 = (bf16[8,12288]{1,0:T(8,128)(2,1)S(1)}, bf16[8,12288]{1,0:T(8,128)(2,1)}, u32[]{:S(2)}) copy-start(bf16[8,12288]{1,0:T(8,128)(2,1)} %cot_h.1) | copy-start | bytes 589828
  7.2 0.9 copy-start.5
  8.1 0.9 copy-start.6
  9.0 0.7 copy-start.7

commit v2 on v1

--- a/solution.py
+++ b/solution.py
@@ -22,6 +22,7 @@
 TN = (((0,), (0,)), ((), ()))
 VMEM = pl.BlockSpec(memory_space=pltpu.VMEM)
 ANY = pl.BlockSpec(memory_space=pl.ANY)
+HBM = pl.BlockSpec(memory_space=pltpu.HBM)
 
 
 def dot(a, b, form=NN):
@@ -109,7 +110,7 @@
     return normed, mixed, (x_ref[...].astype(F32) + dot(mixed, out)).astype(BF16)
 
 
-def attend_back(x, g, mixed, qkv, out, qkv_s, p_s, acc, dm_s, grads, first, n, size):
+def attend_back(x, g, mixed, qkv, out, qkv_s, p_s, acc, dm_s, grads, first, n, size, between):
     dm_s[...] = dot(g, out, NT).astype(BF16)
     put(grads, first + 3, dot(mixed, g, TN))
     acc[...] = jnp.zeros(acc.shape, F32)
@@ -127,7 +128,9 @@
             acc[2, rows] += dot(p.astype(BF16), dm, TN)
         return 0
 
-    lax.fori_loop(0, HEADS, head, 0)
+    for k, step in enumerate(between):
+        lax.fori_loop(k * HEADS // len(between), (k + 1) * HEADS // len(between), head, 0)
+        step()
     hat, scale = norm(x.astype(F32))
     normed = hat.astype(BF16)
     dn = None
@@ -301,7 +304,8 @@
         low, high = s * length, (s + 1) * length
         inside = (row >= low) & (row < high) & (column >= low) & (column < high)
         same = inside if same is None else same | inside
-    bias[...] = jnp.where(same, split[...].astype(F32), 0.0)
+    tiled = jnp.concatenate([split[...].astype(F32)] * (size_s // length), axis=1)
+    bias[...] = jnp.where(same, tiled, 0.0)
     settle(g_copies)
     g_s[...] = moved(at(4), unpack(g_got, flat, few)).astype(BF16)
     settle(f_copies)
@@ -316,10 +320,10 @@
         cdf = 0.5 * (1.0 + lax.erf(pre * (1.0 / math.sqrt(2.0))))
         hidden = (pre * cdf).astype(BF16)
         slope = cdf + pre * (jnp.exp(pre * pre * -0.5) * (1.0 / math.sqrt(2.0 * math.pi)))
-        dh = dot(g, down[c * E:(c + 1) * E], NT).astype(BF16).astype(F32)
+        dh = dot(g, down[:, c * E:(c + 1) * E]).astype(BF16).astype(F32)
         dpre = (dh * slope).astype(BF16)
         put(grads, c, dot(normed, dpre, TN))
-        put(grads, 4 + c, dot(hidden, g, TN))
+        put(grads, 4 + c, dot(g, hidden, TN))
         part = dot(dpre, w_up, NT)
         if c == 0:
             dn_s[...] = part
@@ -332,24 +336,31 @@
     next(ffn)
     dn = dn_s[...].astype(BF16).astype(F32)
     g = (g.astype(F32) + norm_back(hat, scale, dn)).astype(BF16)
+
+    def go(*groups):
+        def step():
+            for group in groups:
+                next(group)
+        return step
+
     back = attend_back(
-        x_s[...], g, mixed, qkvs, outs[...], qkv_s, p_s, acc, dm_s, grads, starts[1], n_s, size_s
+        x_s[...], g, mixed, qkvs, outs[...], qkv_s, p_s, acc, dm_s, grads, starts[1], n_s, size_s,
+        (go(ffn), go(), go(ffn)),
     )
     pack(b_send, moved(at(5), back), few)
     b_copies = start_swap(("rec", "attr"), b_send, b_got, b_sems)
     next(samp)
-    next(ffn)
     settle(b_copies)
-    next(samp)
-    next(ffn)
+    go(samp, ffn)()
     g = moved(at(6), unpack(b_got, flat, few)).astype(BF16)
     back = attend_back(
-        x_a[...], g, mixed_a[...], qkva, outa[...], qkv_a, p_a, acc, dm_s, grads, starts[2], n_a, size_a
-    )
+        x_a[...], g, mixed_a[...], qkva, outa[...], qkv_a, p_a, acc, dm_s, grads, starts[2], n_a, size_a,
+        (go(ffn), go(samp), go(ffn)),
+    )
+    next(attr)
     pack(o_send, back.astype(F32), few)
     o_copies = start_swap(("attr",), o_send, o_got, o_sems)
-    next(attr)
-    for steps in (ffn, samp, attr, ffn, samp, attr, ffn, samp, attr, ffn, samp, attr, samp, attr, attr):
+    for steps in (samp, attr, ffn, samp, attr, samp, attr, samp, attr, attr, attr):
         next(steps)
     settle(o_copies)
 
@@ -381,8 +392,7 @@
         return jnp.concatenate([side[:, :E], side[:, E:]], axis=0)
 
     gu[...] = jnp.concatenate([block(c) for c in range(4)], axis=1)
-    for c in range(4):
-        gd[c * E:(c + 1) * E] = block(4 + c)
+    gd[...] = jnp.concatenate([block(4 + c) for c in range(4)], axis=1)
     for ref, start in ((qs, 8), (qa, 12)):
         ref[...] = jnp.concatenate([block(start + t) for t in range(3)], axis=1)
     os[...] = block(11)
@@ -410,7 +420,7 @@
         place((few, n_rec, n_attr, thin), (0, 2, 1, 3)),
         place((few, n_attr, cols), (2, 1, 0)),
     ]))
-    split = jnp.tile(train_split, size // length)[None, :]
+    split = train_split[None, :]
     all_devices = n_rec * n_attr
     part = E // 2 // n_rec
     n_x = n_attr // 2
@@ -422,7 +432,7 @@
         return pltpu.VMEM(dims, dtype)
 
     args = (
-        cells, cotangent, qkv_attr, out_attr, qkv_samp, out_samp, up_weight, down_weight, split, places
+        cells, cotangent, qkv_attr, out_attr, qkv_samp, out_samp, up_weight, down_weight.T, split, places
     )
     c_buf = vmem(n_attr, cols, few * E)
     g_buf = vmem(n_rec, thin * n_attr, few * E)
@@ -441,7 +451,7 @@
     o_got, totals = pl.pallas_call(
         functools.partial(layer_kernel, width, size, length, few),
         out_shape=[shape(n_attr, cols, few * E), shape(BLOCKS, n_rec, part, 2 * E)],
-        in_specs=[ANY] * len(args),
+        in_specs=[HBM] * len(args),
         out_specs=[VMEM] * 2,
         scratch_shapes=[pltpu.VMEM(a.shape, a.dtype) for a in args]
         + [
@@ -458,13 +468,13 @@
         ]
         + sums,
         compiler_params=pltpu.CompilerParams(
-            collective_id=0, has_side_effects=True, vmem_limit_bytes=48 * 2**20
+            collective_id=0, has_side_effects=True, vmem_limit_bytes=67043328
         ),
     )(*args)
     outs = [
         shape(rows, cols * E), shape(E, 3 * E, dtype=F32), shape(E, E, dtype=F32),
         shape(E, 3 * E, dtype=F32), shape(E, E, dtype=F32),
-        shape(E, 4 * E, dtype=F32), shape(4 * E, E, dtype=F32),
+        shape(E, 4 * E, dtype=F32), shape(E, 4 * E, dtype=F32),
     ]
     last = (o_got, places, totals)
     out = pl.pallas_call(
@@ -477,9 +487,9 @@
             pltpu.SemaphoreType.DMA((3,)), vmem(tokens, E, dtype=F32), vmem(tokens, E, dtype=F32),
             vmem(BLOCKS, E // 2, 2 * E, dtype=F32),
         ],
-        compiler_params=pltpu.CompilerParams(vmem_limit_bytes=48 * 2**20),
+        compiler_params=pltpu.CompilerParams(vmem_limit_bytes=67043328),
     )(*last)
-    return tuple(out)
+    return (*out[:6], out[6].T)
 
 
 def solution(mesh):

time: 91.5 us -> 83.7 us (0.915)
  local copies, waits for them, and re-layouts: 10.1 us -> 0 us
  Pallas kernels: 80.3 us -> 82.7 us
    unnamed x17 -> x0, local copies, waits for them, and re-layouts: 8.33 us -> none
    pallas_call x1, Pallas kernels: 77.4 us -> 79.5 us  [local(): pl.pallas_call(functools.partial(layer_kernel, width, size, length, few),...]
    pallas_call x1 -> x0, local copies, waits for them, and re-layouts: 1.07 us -> none  [local(): pl.pallas_call(functools.partial(finish_kernel, 1.0 / math.sqrt(length *...]
where the time goes in v2:
time: 83.7 us; the launch traced here: 83.5 us
  Pallas kernels  82.7 us (99%)
    pallas_call x1, Pallas kernels, local(): pl.pallas_call(functools.partial(layer_kernel, width, size, length, few),...  79.5 us
    pallas_call x1, Pallas kernels, local(): pl.pallas_call(functools.partial(finish_kernel, 1.0 / math.sqrt(length *...  3.25 us

profile of v2, /device:TPU:0, one launch (start us, length us, event | category | flops | bytes accessed | tf_op | source)
XLA Modules:
  0.0 83.5 jit_solution(16245497038348218289)
XLA Ops:
  0.6 79.5 %shard_map.153 = (bf16[4,64,384]{2,1,0:T(8,128)(2,1)}, bf16[16,4,24,384]{3,2,1,0:T(8,128)(2,1)}) custom-call(bf16[8,12288]{1,0:T(8,128)(2,1)} %cells_h.1, bf16[8,12288]{1,0:T(8,128)(2,1)} %cot_h.1, bf16[192,576]{1,0:T(8,128)(2,1)} %qkva_h.1, bf16[192,192]{1,0:T(8,128)(2,1)} %outa_h.1, bf16[192,576]{1,0:T(8,128)(2,1)} %qkvs_h.1, bf16[192,192]{1,0:T(8,128)(2,1)} %outs_h.1, ...), custom_call_target="tpu_custom_call" | custom-call | tf_op jit(solution)/shard_map/pallas_call | solution.py:451
  80.1 3.2 %shard_map.154 = (bf16[8,12288]{1,0:T(8,128)(2,1)}, f32[192,576]{1,0:T(8,128)}, f32[192,192]{1,0:T(8,128)}, f32[192,576]{1,0:T(8,128)}, f32[192,192]{1,0:T(8,128...) custom-call(bf16[4,64,384]{2,1,0:T(8,128)(2,1)} %get-tuple-element.16.tokens_h, s32[8,512]{1,0:T(8,128)} %constant.2.clone.place_h.places_h, ...), custom_call_target="tpu_custom_call" | custom-call | tf_op jit(solution)/shard_map/pallas_call | solution.py:480

commit v3 on v2

--- a/solution.py
+++ b/solution.py
@@ -81,51 +81,44 @@
     )
 
 
-def head_mask(h):
-    lane = lax.broadcasted_iota(jnp.int32, (1, E), 1)
-    return jnp.where((lane >= h * HD) & (lane < (h + 1) * HD), 1.0, 0.0).astype(F32)
-
-
 def attend(x_ref, qkv, out, qkv_s, p_s, acc, n, size, bias):
     normed = norm(x_ref[...].astype(F32))[0].astype(BF16)
     for t in range(3):
-        qkv_s[t] = dot(normed, qkv[:, t * E:(t + 1) * E]).astype(BF16)
-    acc[0] = jnp.zeros(acc.shape[1:], F32)
+        qkv_s[t] = dot(normed, qkv[:, t * E:(t + 1) * E]).T.astype(BF16)
 
     def head(h, _):
-        mask = head_mask(h)
+        rows = pl.ds(pl.multiple_of(h * HD, HD), HD)
         for b in range(n):
-            rows = pl.ds(b * size, size)
-            s = dot(qkv_s[0, rows] * mask.astype(BF16), qkv_s[1, rows], NT) * SCALE
+            cols = pl.ds(b * size, size)
+            s = dot(qkv_s[1, rows, cols], qkv_s[0, rows, cols], TN) * SCALE
             if bias is not None:
                 s = jnp.where(bias[...] > 0, s, -1e30)
-            e = jnp.exp(s - jnp.max(s, axis=-1, keepdims=True))
-            p = e * (1.0 / jnp.sum(e, axis=-1, keepdims=True))
+            e = jnp.exp(s - jnp.max(s, axis=0, keepdims=True))
+            p = e * (1.0 / jnp.sum(e, axis=0, keepdims=True))
             p_s[b, h] = p
-            acc[0, rows] += dot(p.astype(BF16), qkv_s[2, rows]) * mask
+            acc[0, rows, cols] = dot(qkv_s[2, rows, cols], p.astype(BF16))
         return 0
 
     lax.fori_loop(0, HEADS, head, 0)
-    mixed = acc[0].astype(BF16)
+    mixed = acc[0].T.astype(BF16)
     return normed, mixed, (x_ref[...].astype(F32) + dot(mixed, out)).astype(BF16)
 
 
 def attend_back(x, g, mixed, qkv, out, qkv_s, p_s, acc, dm_s, grads, first, n, size, between):
-    dm_s[...] = dot(g, out, NT).astype(BF16)
+    dm_s[...] = dot(out, g, NT).astype(BF16)
     put(grads, first + 3, dot(mixed, g, TN))
-    acc[...] = jnp.zeros(acc.shape, F32)
 
     def head(h, _):
-        mask = head_mask(h)
+        rows = pl.ds(pl.multiple_of(h * HD, HD), HD)
         for b in range(n):
-            rows = pl.ds(b * size, size)
-            dm = dm_s[rows] * mask.astype(BF16)
+            cols = pl.ds(b * size, size)
+            dm = dm_s[rows, cols]
             p = p_s[b, h]
-            dp = dot(dm, qkv_s[2, rows], NT).astype(BF16).astype(F32)
-            ds = (p * (dp - jnp.sum(dp * p, axis=-1, keepdims=True)) * SCALE).astype(BF16)
-            acc[0, rows] += dot(ds, qkv_s[1, rows]) * mask
-            acc[1, rows] += dot(ds, qkv_s[0, rows], TN) * mask
-            acc[2, rows] += dot(p.astype(BF16), dm, TN)
+            dp = dot(qkv_s[2, rows, cols], dm, TN).astype(BF16).astype(F32)
+            ds = (p * (dp - jnp.sum(dp * p, axis=0, keepdims=True)) * SCALE).astype(BF16)
+            acc[0, rows, cols] = dot(qkv_s[1, rows, cols], ds)
+            acc[1, rows, cols] = dot(qkv_s[0, rows, cols], ds, NT)
+            acc[2, rows, cols] = dot(dm, p.astype(BF16), NT)
         return 0
 
     for k, step in enumerate(between):
@@ -135,7 +128,7 @@
     normed = hat.astype(BF16)
     dn = None
     for t in range(3):
-        d = acc[t].astype(BF16)
+        d = acc[t].T.astype(BF16)
         put(grads, first + t, dot(normed, d, TN))
         part = dot(d, qkv[:, t * E:(t + 1) * E], NT)
         dn = part if dn is None else dn + part
@@ -305,7 +298,7 @@
         inside = (row >= low) & (row < high) & (column >= low) & (column < high)
         same = inside if same is None else same | inside
     tiled = jnp.concatenate([split[...].astype(F32)] * (size_s // length), axis=1)
-    bias[...] = jnp.where(same, tiled, 0.0)
+    bias[...] = jnp.where(same, tiled, 0.0).T
     settle(g_copies)
     g_s[...] = moved(at(4), unpack(g_got, flat, few)).astype(BF16)
     settle(f_copies)
@@ -457,9 +450,9 @@
         + [
             pltpu.SemaphoreType.DMA((len(args),)),
             vmem(tokens, E, dtype=F32), c_buf, c_buf, g_buf, g_buf, f_buf, f_buf, f_buf, f_buf, c_buf,
-            table, table, vmem(3, tokens, E), vmem(tokens // width, HEADS, width, width, dtype=F32),
-            table, table, vmem(3, tokens, E), vmem(tokens // size, HEADS, size, size, dtype=F32),
-            vmem(3, tokens, E, dtype=F32), table, vmem(tokens, E, dtype=F32),
+            table, table, vmem(3, E, tokens), vmem(tokens // width, HEADS, width, width, dtype=F32),
+            table, table, vmem(3, E, tokens), vmem(tokens // size, HEADS, size, size, dtype=F32),
+            vmem(3, E, tokens, dtype=F32), vmem(E, tokens), vmem(tokens, E, dtype=F32),
             vmem(size, size, dtype=F32), vmem(BLOCKS, n_rec, part, 2 * E),
         ]
         + [

time: 83.7 us -> 81.5 us (0.974)
  Pallas kernels: 82.7 us -> 80.6 us
    pallas_call x1, Pallas kernels: 79.5 us -> 77.3 us  [local(): pl.pallas_call(functools.partial(layer_kernel, width, size, length, few),...]
where the time goes in v3:
time: 81.5 us; the launch traced here: 81.4 us
  Pallas kernels  80.6 us (99%)
    pallas_call x1, Pallas kernels, local(): pl.pallas_call(functools.partial(layer_kernel, width, size, length, few),...  77.3 us
    pallas_call x1, Pallas kernels, local(): pl.pallas_call(functools.partial(finish_kernel, 1.0 / math.sqrt(length *...  3.25 us

profile of v3, /device:TPU:0, one launch (start us, length us, event | category | flops | bytes accessed | tf_op | source)
XLA Modules:
  0.0 81.4 jit_solution(15673744628629907534)
XLA Ops:
  0.6 77.3 %shard_map.153 = (bf16[4,64,384]{2,1,0:T(8,128)(2,1)}, bf16[16,4,24,384]{3,2,1,0:T(8,128)(2,1)}) custom-call(bf16[8,12288]{1,0:T(8,128)(2,1)} %cells_h.1, bf16[8,12288]{1,0:T(8,128)(2,1)} %cot_h.1, bf16[192,576]{1,0:T(8,128)(2,1)} %qkva_h.1, bf16[192,192]{1,0:T(8,128)(2,1)} %outa_h.1, bf16[192,576]{1,0:T(8,128)(2,1)} %qkvs_h.1, bf16[192,192]{1,0:T(8,128)(2,1)} %outs_h.1, ...), custom_call_target="tpu_custom_call" | custom-call | tf_op jit(solution)/shard_map/pallas_call | solution.py:444
  78.0 3.2 %shard_map.154 = (bf16[8,12288]{1,0:T(8,128)(2,1)}, f32[192,576]{1,0:T(8,128)}, f32[192,192]{1,0:T(8,128)}, f32[192,576]{1,0:T(8,128)}, f32[192,192]{1,0:T(8,128...) custom-call(bf16[4,64,384]{2,1,0:T(8,128)(2,1)} %get-tuple-element.16.tokens_h, s32[8,512]{1,0:T(8,128)} %constant.2.clone.place_h.places_h, ...), custom_call_target="tpu_custom_call" | custom-call | tf_op jit(solution)/shard_map/pallas_call | solution.py:473
